TPU v7x, 512 devices: a whole 4x8x8 slice. The times are simulated.
512 devices in a mesh: head: 8 (over x, core), blk: 64 (over y, z).
Axes of the slice: x: 4, y: 8, z: 8, core: 2. Of those that a mesh axis runs over, the one named last changes fastest.
Arguments:
- suffix_hidden: bfloat16 [1536, 2048], P('blk'), may hold values from -400 to 400
- prefix_hidden: bfloat16 [16384, 2048], P('blk'), may hold values from -400 to 400
- kv_cache: bfloat16 [2, 16384, 8, 256], P(None, 'blk', 'head'), may hold values from -300 to 300
- norm_gain: float32 [2048], replicated, may hold values from 0.1 to 1.9
- norm_bias: float32 [2048], replicated, may hold values from -3 to 3
- qkv_weight: bfloat16 [2048, 8, 768], P('blk', 'head'), may hold values from -0.125 to 0.125
- qkv_bias: float32 [8, 768], P('head'), may hold values from -3 to 3
- out_weight: bfloat16 [8, 256, 2048], P('head', 'blk'), may hold values from -0.125 to 0.125
- out_bias: float32 [2048], replicated, may hold values from -3 to 3
- suffix_lengths: int32 [4], replicated, may hold values from 1 to 768, 1536 in all
- prefix_blocks: int32 [4], replicated, may hold values from 1 to 32, 64 in all
- block_owner: int32 [64], replicated, may hold values from 0 to 63, each once
- recompute_flag: int32 [16384], P('blk'), may hold values from 0 to 1, as said below
Outputs:
- attn_out: bfloat16 [1536, 2048], P('blk', 'head')
Inputs may be any that keep to these rules, and one draw needn't show every extreme that they name: `recompute_flag`: each storage block of 256 cache rows holds exactly 25 ones.
All inputs are finite; a program needn't handle non-finite values.
Results may differ from a plain program's by a relative error of at most 0.015.
Values may be sent and summed in bfloat16 or wider, within the bound.
A program may use at most 64 MiB of HBM per device.

v0:
```python
import math
import jax
import jax.numpy as jnp
from jax import lax
from jax.sharding import PartitionSpec as P

FLAG_DEV = 25
EPSILON = 1e-05
MASKED = -1e30


def layer_norm(states, norm_scale, norm_shift):
    widened = states.astype(jnp.float32)
    average = jnp.mean(widened, axis=-1, keepdims=True)
    center = widened - average
    variance = jnp.mean(center * center, axis=-1, keepdims=True)
    return (center * lax.rsqrt(variance + EPSILON) * norm_scale + norm_shift).astype(jnp.bfloat16)


def body(
    suffix_hidden,
    prefix_hidden,
    kv_cache,
    norm_gain,
    norm_bias,
    qkv_weight,
    qkv_bias,
    out_weight,
    out_bias,
    suffix_lengths,
    prefix_blocks,
    block_owner,
    recompute_flag,
):
    blk_total = lax.axis_size("blk")
    own_index = lax.axis_index("blk")
    row_count = suffix_hidden.shape[0]
    cache_rows = prefix_hidden.shape[0]
    heads_dev = qkv_weight.shape[1]
    head_dim = qkv_weight.shape[2] // 3
    total_rows = row_count * blk_total
    own_first = own_index * row_count
    tenant_ends = jnp.cumsum(suffix_lengths)
    row_ids = jnp.arange(total_rows, dtype=jnp.int32)
    row_tenant = jnp.sum((row_ids[:, None] >= tenant_ends[None, :]).astype(jnp.int32), axis=1)
    block_ends = jnp.cumsum(prefix_blocks)
    block_slots = jnp.arange(blk_total, dtype=jnp.int32)
    global_block = jnp.sum(jnp.where(block_owner == own_index, block_slots, 0))
    block_tenant = jnp.sum((global_block >= block_ends).astype(jnp.int32))
    normed = layer_norm(suffix_hidden, norm_gain, norm_bias)
    flagged = jnp.argsort(1 - recompute_flag, stable=True)[:FLAG_DEV]
    prefix_normed = layer_norm(prefix_hidden[flagged], norm_gain, norm_bias)
    qkv_rows = qkv_weight.shape[0]
    out_rows = out_weight.shape[1]
    model_dim = out_weight.shape[2]
    packed_weights = jnp.concatenate([qkv_weight.reshape(1, -1), out_weight.reshape(1, -1)], axis=1)
    fetched_all = lax.all_gather(packed_weights, "blk", axis=0, tiled=True)
    qkv_size = qkv_rows * heads_dev * 3 * head_dim
    fetched = fetched_all[:, :qkv_size].reshape(blk_total * qkv_rows, heads_dev, 3 * head_dim)
    out_fetched = fetched_all[:, qkv_size:].reshape(blk_total, heads_dev, out_rows, model_dim)
    out_fetched = jnp.transpose(out_fetched, (1, 0, 2, 3)).reshape(
        heads_dev, blk_total * out_rows, model_dim
    )
    piece_rows = fetched.shape[0]
    flattened = fetched.reshape(piece_rows, heads_dev * 3 * head_dim)
    kv_part = fetched[:, :, head_dim:].reshape(piece_rows, heads_dev * 2 * head_dim)
    suffix_acc = jnp.dot(normed, flattened, preferred_element_type=jnp.float32)
    prefix_acc = jnp.dot(prefix_normed, kv_part, preferred_element_type=jnp.float32)
    suffix_acc, prefix_acc = (suffix_acc, prefix_acc)
    projected = (
        (suffix_acc + qkv_bias.reshape(-1))
        .astype(jnp.bfloat16)
        .reshape(row_count, heads_dev, 3 * head_dim)
    )
    recomputed = (
        (prefix_acc + qkv_bias[:, head_dim:].reshape(-1))
        .astype(jnp.bfloat16)
        .reshape(FLAG_DEV, heads_dev, 2 * head_dim)
    )
    own_queries = projected[:, :, :head_dim].reshape(row_count, heads_dev * head_dim)
    gathered = lax.all_gather(own_queries, "blk", axis=0, tiled=True)
    prefix_keys = kv_cache[0].at[flagged].set(recomputed[:, :, :head_dim])
    prefix_values = kv_cache[1].at[flagged].set(recomputed[:, :, head_dim:])
    keys_all = jnp.concatenate([prefix_keys, projected[:, :, head_dim : 2 * head_dim]], axis=0)
    values_all = jnp.concatenate([prefix_values, projected[:, :, 2 * head_dim :]], axis=0)
    own_tenant = lax.dynamic_slice_in_dim(row_tenant, own_first, row_count, 0)
    key_tenant = jnp.concatenate([jnp.full((cache_rows,), block_tenant, jnp.int32), own_tenant])
    key_position = jnp.concatenate(
        [jnp.full((cache_rows,), -1, jnp.int32), own_first + jnp.arange(row_count, dtype=jnp.int32)]
    )
    scale = head_dim ** (-0.5)
    qblock = math.gcd(total_rows, 512)
    block_total = total_rows // qblock

    def partial_block(offset):
        query_block = lax.dynamic_slice_in_dim(gathered, offset, qblock, 0).reshape(
            qblock, heads_dev, head_dim
        )
        query_tenant = lax.dynamic_slice_in_dim(row_tenant, offset, qblock, 0)
        query_position = offset + jnp.arange(qblock, dtype=jnp.int32)
        allowed = (query_tenant[:, None] == key_tenant[None, :]) & (
            key_position[None, :] <= query_position[:, None]
        )
        scores = (
            jnp.einsum("qhd,khd->hqk", query_block, keys_all, preferred_element_type=jnp.float32)
            * scale
        )
        gate = allowed[None, :, :]
        row_peak = jnp.max(jnp.where(gate, scores, MASKED), axis=2)
        weights = jnp.where(gate, jnp.exp(scores - row_peak[:, :, None]), 0.0)
        denominator = jnp.sum(weights, axis=2)
        numerator = jnp.einsum(
            "hqk,khd->qhd",
            weights.astype(jnp.bfloat16),
            values_all,
            preferred_element_type=jnp.float32,
        )
        return (numerator.reshape(qblock, heads_dev * head_dim), denominator.T, row_peak.T)

    def fill_block(step_index, buffers):
        numer_buf, denom_buf, peak_buf = buffers
        offset = step_index * qblock
        numerator, denominator, row_peak = partial_block(offset)
        numer_buf = lax.dynamic_update_slice_in_dim(numer_buf, numerator, offset, 0)
        denom_buf = lax.dynamic_update_slice_in_dim(denom_buf, denominator, offset, 0)
        peak_buf = lax.dynamic_update_slice_in_dim(peak_buf, row_peak, offset, 0)
        return (numer_buf, denom_buf, peak_buf)

    initial = (
        jnp.zeros((total_rows, heads_dev * head_dim), jnp.float32),
        jnp.zeros((total_rows, heads_dev), jnp.float32),
        jnp.full((total_rows, heads_dev), MASKED, jnp.float32),
    )
    numer_buf, denom_buf, peak_buf = lax.fori_loop(0, block_total, fill_block, initial)
    width = heads_dev * head_dim + 2 * heads_dev
    packed = jnp.concatenate([numer_buf, denom_buf, peak_buf], axis=1).reshape(
        blk_total, row_count * width
    )
    received = lax.all_to_all(packed, "blk", split_axis=0, concat_axis=0, tiled=True)
    received = received.reshape(blk_total, row_count, width)
    recv_numer = received[:, :, : heads_dev * head_dim]
    recv_denom = received[:, :, heads_dev * head_dim : heads_dev * head_dim + heads_dev]
    recv_peak = received[:, :, heads_dev * head_dim + heads_dev :]
    best = jnp.max(recv_peak, axis=0)
    factor = jnp.exp(recv_peak - best[None])
    summed_denom = jnp.sum(factor * recv_denom, axis=0)
    summed_numer = jnp.sum(
        recv_numer.reshape(blk_total, row_count, heads_dev, head_dim) * factor[:, :, :, None],
        axis=0,
    )
    attended = (summed_numer / summed_denom[:, :, None]).astype(jnp.bfloat16)
    mixed = jnp.einsum("rhd,hde->re", attended, out_fetched, preferred_element_type=jnp.float32)
    head_total = lax.axis_size("head")
    columns = mixed.shape[1] // head_total
    pieces = mixed.astype(jnp.bfloat16).reshape(row_count, head_total, columns)
    pieces = jnp.transpose(pieces, (1, 0, 2))
    exchanged = lax.all_to_all(pieces, "head", split_axis=0, concat_axis=0, tiled=True)
    summed = jnp.sum(exchanged.astype(jnp.float32), axis=0)
    bias_part = lax.dynamic_slice_in_dim(out_bias, lax.axis_index("head") * columns, columns, 0)
    return (summed + bias_part).astype(jnp.bfloat16)


def solution(mesh):
    return jax.shard_map(
        body,
        mesh=mesh,
        in_specs=(
            P("blk", None),
            P("blk", None),
            P(None, "blk", "head", None),
            P(),
            P(),
            P("blk", "head", None),
            P("head", None),
            P("head", "blk", None),
            P(),
            P(),
            P(),
            P(),
            P("blk"),
        ),
        out_specs=P("blk", "head"),
        check_vma=False,
    )
```

profile of v0, /device:TPU:8, one launch (start us, length us, event | category | flops | bytes accessed | tf_op | source)
XLA Modules:
  0.0 287.5 jit_solution(16090769834102768445)
XLA Ops:
  11.6 1.4 fusion.49
  13.0 1.3 fusion.50
  16.3 3.2 %sort.17 = (s32[256]{0:T(256)}, s32[256]{0:T(256)S(1)}) sort(s32[256]{0:T(256)S(1)} %broadcast_subtract_fusion, s32[256]{0:T(256)S(1)} %iota.25), dimensions={0}, to_apply=%region_7.8 | sort | flops 2048 | bytes 4096 | tf_op jit(solution)/shard_map/jit(argsort)/sort | solution.py:51
  21.3 1.1 fusion.29
  22.6 91.7 %all-gather.4.cloned.1.call-done = bf16[64,1,32768]{2,1,0:T(2,128)(2,1)} async-done(((bf16[1,1,32768]{2,1,0:T(2,128)(2,1)}), bf16[64,1,32768]{2,1,0:T(2,128)(2,1)}) %all-gather.4.cloned.1.call-update) | async-done | bytes 4194320 | tf_op jit(solution)/shard_map/all_gather | solution.py:57
  114.3 7.9 %copy.55 = bf16[64,1,32768]{2,0,1:T(8,128)(2,1)S(1)} copy(bf16[64,1,32768]{2,1,0:T(2,128)(2,1)} %all-gather.4.cloned.1.call-done) | data formatting | bytes 8388608
  122.2 1.9 copy-done.1
  124.2 1.9 slice.62
  126.0 4.8 %reshape_reshape.3 = bf16[2048,768]{1,0:T(8,128)(2,1)} reshape(bf16[64,24576]{1,0:T(8,128)(2,1)} %slice.62) | data formatting | bytes 6291456 | tf_op jit(solution)/shard_map/reshape;reshape | solution.py:65
  130.9 4.9 %reshape.221 = bf16[2048,1,768]{2,0,1:T(8,128)(2,1)} reshape(bf16[64,24576]{1,0:T(8,128)(2,1)} %slice.62) | data formatting | bytes 6291456 | tf_op jit(solution)/shard_map/reshape | solution.py:59
  135.8 2.6 fusion.19
  138.5 49.4 %all-gather = bf16[1536,1,256]{2,0,1:T(8,128)(2,1)S(1)} all-gather(bf16[24,1,256]{2,0,1:T(8,128)(2,1)S(1)} %get-tuple-element.212), channel_id=2, replica_groups=mesh['head'=8,'blk'=64] {'blk'}, dimensions={0}, use_global_device_ids=true | all-gather | bytes 798720 | tf_op jit(solution)/shard_map/all_gather | solution.py:81
  192.1 11.9 %while.17 = (s32[]{:T(128)}, f32[1536,256]{1,0:T(8,128)S(1)}, f32[1536,1]{0,1:T(1,128)}, f32[1536,1]{0,1:T(1,128)}, s32[1536]{0:T(1024)}, /*index=5*/s32[280]{0:...) while((s32[]{:T(128)}, f32[1536,256]{1,0:T(8,128)S(1)}, ...), condition=%wide.region_15.16_spmd, body=%wide.region_12.15_spmd.sunk | while | flops 149380608 | bytes 2841579 | solution.py:134
  193.9 1.4 convolution_dynamic-update-slice_fusion.2
  197.8 1.4 convolution_dynamic-update-slice_fusion.2
  201.8 1.4 convolution_dynamic-update-slice_fusion.2
  204.0 1.9 copy.40
  205.9 1.9 copy.39
  207.8 2.2 pad_maximum_fusion
  210.0 4.3 %all_to_all.12 = f32[64,1,6192]{2,1,0:T(1,128)} reshape(f32[1536,258]{1,0:T(8,128)S(1)} %pad_maximum_fusion) | data formatting | bytes 3170304 | tf_op jit(solution)/shard_map/all_to_all | solution.py:139
  214.3 10.0 %all-to-all-start = ((f32[64,1,6192]{2,1,0:T(1,128)}), f32[64,1,6192]{2,1,0:T(1,128)S(1)}, u32[]{:S(2)}, u32[]{:S(2)}) async-start(f32[64,1,6192]{2,1,0:T(1,128)} %all_to_all.12), calls=%async_computation | async-start | bytes 3211264 | tf_op jit(solution)/shard_map/all_to_all | solution.py:139
  224.3 2.3 slice.72
  226.6 2.7 reshape.225
  229.3 25.7 %all-to-all-done = f32[64,1,6192]{2,1,0:T(1,128)S(1)} async-done(((f32[64,1,6192]{2,1,0:T(1,128)}), f32[64,1,6192]{2,1,0:T(1,128)S(1)}, u32[]{:S(2)}, u32[]{:S(2)}) %all-to-all-start) | async-done | bytes 1585184 | tf_op jit(solution)/shard_map/all_to_all | solution.py:139
  255.0 5.4 %reduce.14 = f32[64,6192]{1,0:T(8,128)} reduce(f32[64,1,6192]{2,1,0:T(1,128)S(1)} %all-to-all-done, f32[]{:T(128)} %constant.108), dimensions={1}, to_apply=%all_to_all.10.reduce_sub_computation | reduce | bytes 3170308 | tf_op jit(solution)/shard_map/all_to_all | solution.py:139
  260.4 2.5 reshape.224
  262.9 1.5 fusion.51
  264.4 1.4 copy.48
  265.8 1.4 copy.47
  267.8 1.5 convolution_convert_fusion
  270.0 4.3 %all-to-all-start.1 = ((bf16[8,24,256]{2,1,0:T(8,128)(2,1)}), bf16[8,24,256]{2,1,0:T(8,128)(2,1)S(1)}, u32[]{:S(2)}, u32[]{:S(2)}) async-start(bf16[8,24,256]{2,1,0:T(8,128)(2,1)} %bitcast.70), calls=%async_computation.1 | async-start | bytes 196608 | tf_op jit(solution)/shard_map/all_to_all | solution.py:157
  275.0 5.0 %all-to-all-done.1 = bf16[8,24,256]{2,1,0:T(8,128)(2,1)S(1)} async-done(((bf16[8,24,256]{2,1,0:T(8,128)(2,1)}), bf16[8,24,256]{2,1,0:T(8,128)(2,1)S(1)}, u32[]{:S(2)}, u32[]{:S(2)}) %all-to-all-start.1) | async-done | bytes 98336 | tf_op jit(solution)/shard_map/all_to_all | solution.py:157
  (81 shorter events, 23.6 us)
Async XLA Ops:
  6.5 12.9 %copy-start = (bf16[256,2048]{1,0:T(8,128)(2,1)S(1)}, bf16[256,2048]{1,0:T(8,128)(2,1)}, u32[]{:S(2)}) copy-start(bf16[256,2048]{1,0:T(8,128)(2,1)} %param.16) | copy-start | bytes 3145732
  6.5 16.1 %copy-start.5 = (bf16[2,256,1,256]{3,1,2,0:T(8,128)(2,1)S(1)}, bf16[2,256,1,256]{3,1,2,0:T(8,128)(2,1)}, u32[]{:S(2)}) copy-start(bf16[2,256,1,256]{3,1,2,0:T(8,128)(2,1)} %param.17) | copy-start | bytes 786436
  6.5 107.8 %all-gather.4.cloned.1.call-start = ((), (), s32[]{:S(2)}) async-start(), calls=%async_computation.2 | async-start | bytes 8519680 | tf_op jit(solution)/shard_map/all_gather | solution.py:57
  11.5 1.5 copy-start.7
  122.2 1.9 copy-start.1
  130.9 4.9 %copy-start.4 = (bf16[24,2048]{1,0:T(8,128)(2,1)S(1)}, bf16[24,2048]{1,0:T(8,128)(2,1)}, u32[]{:S(2)}) copy-start(bf16[24,2048]{1,0:T(8,128)(2,1)} %param.15) | copy-start | bytes 294916
  130.9 4.9 %copy-start.8 = (f32[2048]{0:T(1024)S(1)}, f32[2048]{0:T(1024)}, u32[]{:S(2)}) copy-start(f32[2048]{0:T(1024)} %param.19) | copy-start | bytes 24580
  130.9 4.9 %copy-start.9 = (f32[2048]{0:T(1024)S(1)}, f32[2048]{0:T(1024)}, u32[]{:S(2)}) copy-start(f32[2048]{0:T(1024)} %param.18) | copy-start | bytes 24580
  135.8 52.0 %copy-start.3 = (bf16[2048,1,768]{2,0,1:T(8,128)(2,1)S(1)}, bf16[2048,1,768]{2,0,1:T(8,128)(2,1)}, u32[]{:S(2)}) copy-start(bf16[2048,1,768]{2,0,1:T(8,128)(2,1)} %reshape.221) | copy-start | bytes 9437188
  135.8 52.0 %slice-start = ((f32[1,768]{1,0:T(1,128)}), f32[1,512]{1,0:T(1,128)S(1)}, s32[]{:S(2)}) async-start(f32[1,768]{1,0:T(1,128)} %param.21), calls=%async_computation.3 | async-start | bytes 4096 | tf_op jit(solution)/shard_map/slice | solution.py:76
  192.1 3.1 %copy-start.6 = (s32[280]{0:T(512)S(1)}, s32[280]{0:T(512)}, u32[]{:S(2)}) copy-start(s32[280]{0:T(512)} %get-tuple-element.320) | copy-start | bytes 3364 | tf_op jit(solution)/shard_map/while
  196.1 3.1 %copy-start.6 = (s32[280]{0:T(512)S(1)}, s32[280]{0:T(512)}, u32[]{:S(2)}) copy-start(s32[280]{0:T(512)} %get-tuple-element.320) | copy-start | bytes 3364 | tf_op jit(solution)/shard_map/while
  200.0 3.2 %copy-start.6 = (s32[280]{0:T(512)S(1)}, s32[280]{0:T(512)}, u32[]{:S(2)}) copy-start(s32[280]{0:T(512)} %get-tuple-element.320) | copy-start | bytes 3364 | tf_op jit(solution)/shard_map/while
  204.0 3.8 %copy-start.2 = (f32[1536,256]{1,0:T(8,128)}, f32[1536,256]{1,0:T(8,128)S(1)}, u32[]{:S(2)}) copy-start(f32[1536,256]{1,0:T(8,128)S(1)} %get-tuple-element.178) | copy-start | bytes 4718596
  214.3 40.7 %all-to-all-start = ((f32[64,1,6192]{2,1,0:T(1,128)}), f32[64,1,6192]{2,1,0:T(1,128)S(1)}, u32[]{:S(2)}, u32[]{:S(2)}) async-start(f32[64,1,6192]{2,1,0:T(1,128)} %all_to_all.12), calls=%async_computation | async-start | bytes 3211264 | tf_op jit(solution)/shard_map/all_to_all | solution.py:139
  270.0 10.1 %all-to-all-start.1 = ((bf16[8,24,256]{2,1,0:T(8,128)(2,1)}), bf16[8,24,256]{2,1,0:T(8,128)(2,1)S(1)}, u32[]{:S(2)}, u32[]{:S(2)}) async-start(bf16[8,24,256]{2,1,0:T(8,128)(2,1)} %bitcast.70), calls=%async_computation.1 | async-start | bytes 196608 | tf_op jit(solution)/shard_map/all_to_all | solution.py:157
Sparse Core Ops, SparseCore 0:
  10.4 103.9 all-gather.3
where the time goes:
time: 289 us; the launch traced here: 288 us
  waiting for transfers between devices  122 us (42%)
  local copies, waits for them, and re-layouts  52.2 us (18%)
  blocking collectives  49.4 us (17%)
  other arithmetic  23.7 us (8%)
  starting transfers between devices  14.3 us (5%)
  between operations  13.6 us (5%)
  matrix products  11.7 us (4%)
    all_gather x1, waiting for transfers between devices, body(): fetched_all = lax.all_gather(packed_weights, 'blk', axis=0, tiled=True)  91.7 us
    all_gather x1, blocking collectives, body(): gathered = lax.all_gather(own_queries, 'blk', axis=0, tiled=True)  49.4 us
    all_to_all x1, waiting for transfers between devices, body(): lax.all_to_all(packed, 'blk', split_axis=0, concat_axis=0, tiled=True)  25.7 us
    unnamed x23, local copies, waits for them, and re-layouts  14.4 us
    all_to_all x1, starting transfers between devices, body(): lax.all_to_all(packed, 'blk', split_axis=0, concat_axis=0, tiled=True)  10 us
  transfers between devices with their start and end apart: 3, of which 3 were waited for; matrix products, arithmetic and copies ran while one was open for 7% of the time, Pallas kernels for 0%

commit v1 on v0

--- a/solution.py
+++ b/solution.py
@@ -78,7 +78,11 @@
         .reshape(FLAG_DEV, heads_dev, 2 * head_dim)
     )
     own_queries = projected[:, :, :head_dim].reshape(row_count, heads_dev * head_dim)
-    gathered = lax.all_gather(own_queries, "blk", axis=0, tiled=True)
+    size = lax.axis_size("blk")
+    repeats = [size if d == 0 else 1 for d in range(own_queries.ndim)]
+    gathered = lax.all_to_all(
+        jnp.tile(own_queries, repeats), "blk", split_axis=0, concat_axis=0, tiled=True
+    )
     prefix_keys = kv_cache[0].at[flagged].set(recomputed[:, :, :head_dim])
     prefix_values = kv_cache[1].at[flagged].set(recomputed[:, :, head_dim:])
     keys_all = jnp.concatenate([prefix_keys, projected[:, :, head_dim : 2 * head_dim]], axis=0)

time: 289 us -> 274 us (0.948)
  the two profiles are of different devices: /device:TPU:8 before, /device:TPU:1 now
where the time goes in v1:
time: 274 us; the launch traced here: 273 us
  waiting for transfers between devices  142 us (52%)
  local copies, waits for them, and re-layouts  53.1 us (19%)
  starting transfers between devices  27.6 us (10%)
  other arithmetic  23.7 us (9%)
  between operations  13.6 us (5%)
  matrix products  13.2 us (5%)
    all_gather x1, waiting for transfers between devices, body(): fetched_all = lax.all_gather(packed_weights, 'blk', axis=0, tiled=True)  93.7 us
    all_to_all x1, waiting for transfers between devices, body(): lax.all_to_all(packed, 'blk', split_axis=0, concat_axis=0, tiled=True)  32.9 us
    unnamed x21, local copies, waits for them, and re-layouts  14.4 us
    all_to_all x1, waiting for transfers between devices, body(): lax.all_to_all(jnp.tile(own_queries, repeats), 'blk', split_axis=0, conca...  10.7 us
    all_to_all x1, starting transfers between devices, body(): lax.all_to_all(jnp.tile(own_queries, repeats), 'blk', split_axis=0, conca...  9.79 us
    all_to_all x1, starting transfers between devices, body(): lax.all_to_all(packed, 'blk', split_axis=0, concat_axis=0, tiled=True)  9.26 us
    all_to_all x1, starting transfers between devices, body(): lax.all_to_all(pieces, 'head', split_axis=0, concat_axis=0, tiled=True)  8.58 us
  transfers between devices with their start and end apart: 4, of which 4 were waited for; matrix products, arithmetic and copies ran while one was open for 10% of the time, Pallas kernels for 0%

profile of v1, /device:TPU:1, one launch (start us, length us, event | category | flops | bytes accessed | tf_op | source)
XLA Modules:
  0.0 272.9 jit_solution(16990334677357716392)
XLA Ops:
  11.6 1.4 fusion.49
  16.2 3.2 %sort.17 = (s32[256]{0:T(256)}, s32[256]{0:T(256)S(1)}) sort(s32[256]{0:T(256)S(1)} %broadcast_subtract_fusion, s32[256]{0:T(256)S(1)} %iota.25), dimensions={0}, to_apply=%region_7.8 | sort | flops 2048 | bytes 4096 | tf_op jit(solution)/shard_map/jit(argsort)/sort | solution.py:51
  21.6 93.7 %all-gather.3.cloned.1.call-done = bf16[64,1,32768]{2,1,0:T(2,128)(2,1)} async-done(((bf16[1,1,32768]{2,1,0:T(2,128)(2,1)}), bf16[64,1,32768]{2,1,0:T(2,128)(2,1)}) %all-gather.3.cloned.1.call-update) | async-done | bytes 4194320 | tf_op jit(solution)/shard_map/all_gather | solution.py:57
  115.2 7.9 %copy.55 = bf16[64,1,32768]{2,0,1:T(8,128)(2,1)S(1)} copy(bf16[64,1,32768]{2,1,0:T(2,128)(2,1)} %all-gather.3.cloned.1.call-done) | data formatting | bytes 8388608
  123.2 1.9 copy-done.1
  125.1 1.9 slice.62
  127.0 4.9 %reshape_reshape.3 = bf16[2048,768]{1,0:T(8,128)(2,1)} reshape(bf16[64,24576]{1,0:T(8,128)(2,1)} %slice.62) | data formatting | bytes 6291456 | tf_op jit(solution)/shard_map/reshape;reshape | solution.py:65
  131.8 2.5 fusion.19
  135.3 9.8 %all-to-all-start = ((bf16[64,24,256]{2,1,0:T(8,128)(2,1)}), bf16[64,24,256]{2,1,0:T(8,128)(2,1)S(1)}, u32[]{:S(2)}, u32[]{:S(2)}) async-start(bf16[64,24,256]{2,1,0:T(8,128)(2,1)} %tile.9), calls=%async_computation | async-start | bytes 1572864 | tf_op jit(solution)/shard_map/all_to_all | solution.py:83
  146.1 4.8 %reshape.224 = bf16[2048,1,768]{2,0,1:T(8,128)(2,1)} reshape(bf16[64,24576]{1,0:T(8,128)(2,1)} %slice.62) | data formatting | bytes 6291456 | tf_op jit(solution)/shard_map/reshape | solution.py:59
  151.0 2.1 fusion.20
  155.6 10.7 %all-to-all-done = bf16[64,24,256]{2,1,0:T(8,128)(2,1)S(1)} async-done(((bf16[64,24,256]{2,1,0:T(8,128)(2,1)}), bf16[64,24,256]{2,1,0:T(8,128)(2,1)S(1)}, u32[]{:S(2)}, u32[]{:S(2)}) %all-to-all-start) | async-done | bytes 786464 | tf_op jit(solution)/shard_map/all_to_all | solution.py:83
  167.5 11.9 %while.17 = (s32[]{:T(128)}, f32[1536,256]{1,0:T(8,128)S(1)}, f32[1536,1]{0,1:T(1,128)}, f32[1536,1]{0,1:T(1,128)}, s32[1536]{0:T(1024)}, /*index=5*/s32[280]{0:...) while((s32[]{:T(128)}, f32[1536,256]{1,0:T(8,128)S(1)}, ...), condition=%wide.region_15.16_spmd, body=%wide.region_12.15_spmd.sunk | while | flops 149380608 | bytes 2841579 | solution.py:138
  169.3 1.4 convolution_dynamic-update-slice_fusion.2
  173.3 1.4 convolution_dynamic-update-slice_fusion.2
  177.2 1.4 convolution_dynamic-update-slice_fusion.2
  179.4 1.9 copy.40
  181.3 1.9 copy.39
  183.2 2.2 pad_maximum_fusion
  185.4 4.3 %all_to_all.20 = f32[64,1,6192]{2,1,0:T(1,128)} reshape(f32[1536,258]{1,0:T(8,128)S(1)} %pad_maximum_fusion) | data formatting | bytes 3170304 | tf_op jit(solution)/shard_map/all_to_all | solution.py:143
  189.7 9.3 %all-to-all-start.1 = ((f32[64,1,6192]{2,1,0:T(1,128)}), f32[64,1,6192]{2,1,0:T(1,128)S(1)}, u32[]{:S(2)}, u32[]{:S(2)}) async-start(f32[64,1,6192]{2,1,0:T(1,128)} %all_to_all.20), calls=%async_computation.1 | async-start | bytes 3211264 | tf_op jit(solution)/shard_map/all_to_all | solution.py:143
  199.0 2.3 slice.72
  201.2 2.7 reshape.228
  203.9 32.9 %all-to-all-done.1 = f32[64,1,6192]{2,1,0:T(1,128)S(1)} async-done(((f32[64,1,6192]{2,1,0:T(1,128)}), f32[64,1,6192]{2,1,0:T(1,128)S(1)}, u32[]{:S(2)}, u32[]{:S(2)}) %all-to-all-start.1) | async-done | bytes 1585184 | tf_op jit(solution)/shard_map/all_to_all | solution.py:143
  236.9 5.4 %reduce.14 = f32[64,6192]{1,0:T(8,128)} reduce(f32[64,1,6192]{2,1,0:T(1,128)S(1)} %all-to-all-done.1, f32[]{:T(128)} %constant.108), dimensions={1}, to_apply=%all_to_all.18.reduce_sub_computation | reduce | bytes 3170308 | tf_op jit(solution)/shard_map/all_to_all | solution.py:143
  242.2 2.5 reshape.227
  244.8 1.5 fusion.51
  246.3 1.4 copy.48
  247.7 1.4 copy.47
  249.7 1.5 convolution_convert_fusion
  251.9 8.6 %all-to-all-start.2 = ((bf16[8,24,256]{2,1,0:T(8,128)(2,1)}), bf16[8,24,256]{2,1,0:T(8,128)(2,1)S(1)}, u32[]{:S(2)}, u32[]{:S(2)}) async-start(bf16[8,24,256]{2,1,0:T(8,128)(2,1)} %bitcast.72), calls=%async_computation.2 | async-start | bytes 196608 | tf_op jit(solution)/shard_map/all_to_all | solution.py:161
  261.2 4.2 %all-to-all-done.2 = bf16[8,24,256]{2,1,0:T(8,128)(2,1)S(1)} async-done(((bf16[8,24,256]{2,1,0:T(8,128)(2,1)}), bf16[8,24,256]{2,1,0:T(8,128)(2,1)S(1)}, u32[]{:S(2)}, u32[]{:S(2)}) %all-to-all-start.2) | async-done | bytes 98336 | tf_op jit(solution)/shard_map/all_to_all | solution.py:161
  (81 shorter events, 26.4 us)
Async XLA Ops:
  6.5 138.6 %copy-start = (bf16[256,2048]{1,0:T(8,128)(2,1)S(1)}, bf16[256,2048]{1,0:T(8,128)(2,1)}, u32[]{:S(2)}) copy-start(bf16[256,2048]{1,0:T(8,128)(2,1)} %param.16) | copy-start | bytes 3145732
  6.5 108.7 %all-gather.3.cloned.1.call-start = ((), (), s32[]{:S(2)}) async-start(), calls=%async_computation.3 | async-start | bytes 8519680 | tf_op jit(solution)/shard_map/all_gather | solution.py:57
  11.5 1.5 copy-start.6
  123.1 1.9 copy-start.1
  127.0 4.9 %copy-start.3 = (bf16[24,2048]{1,0:T(8,128)(2,1)S(1)}, bf16[24,2048]{1,0:T(8,128)(2,1)}, u32[]{:S(2)}) copy-start(bf16[24,2048]{1,0:T(8,128)(2,1)} %param.15) | copy-start | bytes 294916
  127.0 4.9 %copy-start.7 = (f32[2048]{0:T(1024)S(1)}, f32[2048]{0:T(1024)}, u32[]{:S(2)}) copy-start(f32[2048]{0:T(1024)} %param.19) | copy-start | bytes 24580
  127.0 4.9 %copy-start.8 = (f32[2048]{0:T(1024)S(1)}, f32[2048]{0:T(1024)}, u32[]{:S(2)}) copy-start(f32[2048]{0:T(1024)} %param.18) | copy-start | bytes 24580
  134.3 11.8 %copy-start.4 = (bf16[2,256,1,256]{3,1,2,0:T(8,128)(2,1)S(1)}, bf16[2,256,1,256]{3,1,2,0:T(8,128)(2,1)}, u32[]{:S(2)}) copy-start(bf16[2,256,1,256]{3,1,2,0:T(8,128)(2,1)} %param.17) | copy-start | bytes 786436
  135.3 31.0 %all-to-all-start = ((bf16[64,24,256]{2,1,0:T(8,128)(2,1)}), bf16[64,24,256]{2,1,0:T(8,128)(2,1)S(1)}, u32[]{:S(2)}, u32[]{:S(2)}) async-start(bf16[64,24,256]{2,1,0:T(8,128)(2,1)} %tile.9), calls=%async_computation | async-start | bytes 1572864 | tf_op jit(solution)/shard_map/all_to_all | solution.py:83
  146.1 4.8 %slice-start = ((f32[1,768]{1,0:T(1,128)}), f32[1,512]{1,0:T(1,128)S(1)}, s32[]{:S(2)}) async-start(f32[1,768]{1,0:T(1,128)} %param.21), calls=%async_computation.4 | async-start | bytes 4096 | tf_op jit(solution)/shard_map/slice | solution.py:76
  167.5 3.1 %copy-start.5 = (s32[280]{0:T(512)S(1)}, s32[280]{0:T(512)}, u32[]{:S(2)}) copy-start(s32[280]{0:T(512)} %get-tuple-element.320) | copy-start | bytes 3364 | tf_op jit(solution)/shard_map/while
  171.5 3.1 %copy-start.5 = (s32[280]{0:T(512)S(1)}, s32[280]{0:T(512)}, u32[]{:S(2)}) copy-start(s32[280]{0:T(512)} %get-tuple-element.320) | copy-start | bytes 3364 | tf_op jit(solution)/shard_map/while
  175.4 3.1 %copy-start.5 = (s32[280]{0:T(512)S(1)}, s32[280]{0:T(512)}, u32[]{:S(2)}) copy-start(s32[280]{0:T(512)} %get-tuple-element.320) | copy-start | bytes 3364 | tf_op jit(solution)/shard_map/while
  179.4 3.8 %copy-start.2 = (f32[1536,256]{1,0:T(8,128)}, f32[1536,256]{1,0:T(8,128)S(1)}, u32[]{:S(2)}) copy-start(f32[1536,256]{1,0:T(8,128)S(1)} %get-tuple-element.178) | copy-start | bytes 4718596
  189.7 47.2 %all-to-all-start.1 = ((f32[64,1,6192]{2,1,0:T(1,128)}), f32[64,1,6192]{2,1,0:T(1,128)S(1)}, u32[]{:S(2)}, u32[]{:S(2)}) async-start(f32[64,1,6192]{2,1,0:T(1,128)} %all_to_all.20), calls=%async_computation.1 | async-start | bytes 3211264 | tf_op jit(solution)/shard_map/all_to_all | solution.py:143
  251.9 13.6 %all-to-all-start.2 = ((bf16[8,24,256]{2,1,0:T(8,128)(2,1)}), bf16[8,24,256]{2,1,0:T(8,128)(2,1)S(1)}, u32[]{:S(2)}, u32[]{:S(2)}) async-start(bf16[8,24,256]{2,1,0:T(8,128)(2,1)} %bitcast.72), calls=%async_computation.2 | async-start | bytes 196608 | tf_op jit(solution)/shard_map/all_to_all | solution.py:161
Sparse Core Ops, SparseCore 0:
  10.4 104.8 all-gather.2
